TPU v7x, 512 devices: a whole 4x8x8 slice. The times are simulated.
512 devices in a mesh: cam: 16 (over x_lo, y), space: 32 (over x_hi, z, core).
Axes of the slice: x: 4 (x_hi: 2, x_lo: 2; x = x_hi * 2 + x_lo), y: 8, z: 8, core: 2. Of those that a mesh axis runs over, the one named last changes fastest.
Arguments:
- features: float32 [64, 131072], P(None, ('cam', 'space')), may hold values from -6 to 6
- positions: float32 [3, 131072], P(None, ('cam', 'space')), may hold values from -6144 to 6144, as said below
- spreads: float32 [131072], P(('cam', 'space')), may hold values from 16 to 64
- logits: float32 [131072], P(('cam', 'space')), may hold values from -6 to -2
- camera: float32 [16, 3], replicated, may hold values from -1 to 1
- decoder: bfloat16 [64, 512], replicated, may hold values from -0.75 to 0.75
- tile_lists: int32 [16, 32, 16, 256], P('cam', 'space'), may hold values from 0 to 8191, as said below
- counts: int32 [16, 32, 16], P('cam', 'space'), may hold values from 1 to 256, as said below
- targets: bfloat16 [16, 32, 16, 256, 512], P('cam', 'space'), may hold values from -6 to 6
Outputs:
- grad_features: float32 [64, 131072], P(None, ('cam', 'space'))
- grad_logits: float32 [131072], P(('cam', 'space'))
Inputs may be any that keep to these rules, and one draw needn't show every extreme that they name: `positions`: rows are x, y and depth; depth lies between 4 and 8. `tile_lists`: the list of tile (c, s, j) names only ids j * 256 + q or 4096 + j * 256 + q with 0 <= q < 256, no id twice; lists of tile row 0 name only ids below 4096. `counts`: some tile has all 256 entries live.
All inputs are finite; a program needn't handle non-finite values.
Results may differ from a plain program's by a relative error of at most 0.003.
Values may be sent and summed in bfloat16 or wider, within the bound.
No kernel may reach another device: no remote copies, remote signals or barrier semaphores. Data moves between devices by JAX's collectives and lax.ppermute only.
A program may use at most 64 MiB of HBM per device.

v0:
```python
import jax
import jax.numpy as jnp
from jax import lax
from jax.sharding import PartitionSpec as P

TS = 16


def shifted(shard, axis, by):
    length = lax.axis_size(axis)
    pairs = [(i, i + by) for i in range(length) if 0 <= i + by < length]
    return lax.ppermute(shard, axis, pairs)


def project_terms(
    gathered, viewers, tile_row, columns, live_counts, grad_maker, image_width, image_height
):
    channels = gathered.shape[0] - 5
    tiles_here = gathered.shape[1]
    length = gathered.shape[2]
    step_len = 128
    block_count = length // step_len
    pixel_count = TS * TS
    feature_bf = gathered[:channels].astype(jnp.bfloat16)
    distance = gathered[channels + 2] - 0.05 * viewers[:, 2:3]
    centre_u = (gathered[channels] - 0.75 * TS * viewers[:, 0:1]) / distance + 0.5 * image_width
    centre_v = (
        gathered[channels + 1] - 0.75 * TS * viewers[:, 1:2]
    ) / distance + 0.5 * image_height
    radius = gathered[channels + 3] / distance
    sigmoid_open = jax.nn.sigmoid(gathered[channels + 4])
    opacity = 0.99 * sigmoid_open
    sigmoid_slope = 0.99 * sigmoid_open * (1.0 - sigmoid_open)
    pixel_id = jnp.arange(pixel_count, dtype=jnp.int32)
    pixel_u = (columns[:, None] * TS + pixel_id[None, :] % TS).astype(jnp.float32) + 0.5
    pixel_v = (tile_row * TS + pixel_id // TS).astype(jnp.float32) + 0.5
    alive_mask = (jnp.arange(length, dtype=jnp.int32)[None, :] < live_counts[:, None]).astype(
        jnp.float32
    )
    logit_gate_all = alive_mask * sigmoid_slope
    steps_used = (jnp.max(live_counts) + step_len - 1) // step_len

    def block_terms(first_entry):

        def window_of(source_array):
            return lax.dynamic_slice_in_dim(
                source_array, first_entry, step_len, axis=source_array.ndim - 1
            )

        delta_u = pixel_u[:, :, None] - window_of(centre_u)[:, None, :]
        delta_v = pixel_v[None, :, None] - window_of(centre_v)[:, None, :]
        spread = window_of(radius)[:, None, :]
        falloff = jnp.exp(-(delta_u * delta_u + delta_v * delta_v) / (2.0 * spread * spread))
        opaque = (window_of(opacity) * window_of(alive_mask))[:, None, :] * falloff
        log_keep = jnp.log(1.0 - opaque)
        inner_log = jnp.cumsum(log_keep, axis=2) - log_keep
        return (
            falloff,
            opaque,
            log_keep,
            inner_log,
            window_of(feature_bf),
            window_of(logit_gate_all),
        )

    def forward(position, state_in):
        log_start, feature_sum, starts = state_in
        first_entry = position * step_len
        falloff, opaque, log_keep, inner_log, block_feat, unused = block_terms(first_entry)
        weight = opaque * jnp.exp(log_start[:, :, None] + inner_log)
        feature_sum = feature_sum + jnp.einsum(
            "tpk,ctk->tcp",
            weight.astype(jnp.bfloat16),
            block_feat,
            preferred_element_type=jnp.float32,
        )
        starts = lax.dynamic_update_index_in_dim(starts, log_start, position, 0)
        return (log_start + jnp.sum(log_keep, axis=2), feature_sum, starts)

    initial = (
        jnp.zeros((tiles_here, pixel_count), jnp.float32),
        jnp.zeros((tiles_here, channels, pixel_count), jnp.float32),
        jnp.zeros((block_count, tiles_here, pixel_count), jnp.float32),
    )
    unused_log, feature_sum, starts = lax.fori_loop(0, steps_used, forward, initial)
    composite = feature_sum.astype(jnp.bfloat16)
    pixel_grad = grad_maker(composite).astype(jnp.bfloat16)

    def backward(reverse_turn, state_in):
        behind_sum, feature_grad, logit_grad = state_in
        position = steps_used - 1 - reverse_turn
        first_entry = position * step_len
        falloff, opaque, log_keep, inner_log, block_feat, logit_gate = block_terms(first_entry)
        keep_to = jnp.exp(
            lax.dynamic_index_in_dim(starts, position, 0, keepdims=False)[:, :, None] + inner_log
        )
        weight = opaque * keep_to
        weight_bf = weight.astype(jnp.bfloat16)
        contrib = jnp.einsum(
            "tcp,ctk->tpk", pixel_grad, block_feat, preferred_element_type=jnp.float32
        )
        weighted = weight * contrib
        block_total = jnp.sum(weighted, axis=2)
        behind = behind_sum[:, :, None] + block_total[:, :, None] - jnp.cumsum(weighted, axis=2)
        dopaque = keep_to * contrib - behind / (1.0 - opaque)
        logit_part = logit_gate * jnp.sum(dopaque * falloff, axis=1)
        feature_part = jnp.einsum(
            "tpk,tcp->ctk", weight_bf, pixel_grad, preferred_element_type=jnp.float32
        )
        feature_grad = lax.dynamic_update_slice_in_dim(
            feature_grad, feature_part, first_entry, axis=2
        )
        logit_grad = lax.dynamic_update_slice_in_dim(logit_grad, logit_part, first_entry, axis=1)
        return (behind_sum + block_total, feature_grad, logit_grad)

    initial_back = (
        jnp.zeros((tiles_here, pixel_count), jnp.float32),
        jnp.zeros((channels, tiles_here, length), jnp.float32),
        jnp.zeros((tiles_here, length), jnp.float32),
    )
    unused_behind, feature_grad, logit_grad = lax.fori_loop(0, steps_used, backward, initial_back)
    return (feature_grad, logit_grad)


def full_target_rule(pixel_targets, decoder):
    decoder_wide = decoder.astype(jnp.float32)

    def make_grad(composite):
        decoded = jnp.einsum("tcp,cd->tpd", composite, decoder, preferred_element_type=jnp.float32)
        residual = decoded - pixel_targets.astype(jnp.float32)
        return jnp.einsum("tpd,cd->tcp", residual, decoder_wide, precision=lax.Precision.HIGHEST)

    return make_grad


def on_device(features, positions, spreads, logits, camera, decoder, tile_lists, counts, targets):
    channels = features.shape[0]
    length = features.shape[1]
    camera_count = lax.axis_size("cam")
    space_count = lax.axis_size("space")
    camera_id = lax.axis_index("cam")
    tile_row = lax.axis_index("space")
    image_width = TS * camera_count
    image_height = TS * space_count
    block_rows = camera_count * length
    own_slab = jnp.concatenate([features, positions, spreads[None], logits[None]], axis=0)
    upper_slab = shifted(own_slab, "space", 1)
    both_slabs = lax.all_gather(jnp.stack([own_slab, upper_slab]), "cam", axis=2, tiled=True)
    gauss_table = jnp.concatenate([both_slabs[0], both_slabs[1]], axis=1)
    entries = tile_lists[0, 0]
    picker = (jnp.arange(camera_count, dtype=jnp.int32) == camera_id).astype(jnp.float32)
    viewers = jnp.broadcast_to(jnp.sum(camera * picker[:, None], axis=0), (camera_count, 3))
    columns = jnp.arange(camera_count, dtype=jnp.int32)
    gathered = jnp.take(gauss_table, entries, axis=1)
    grad_maker = full_target_rule(targets[0, 0], decoder)
    feature_grad, logit_grad = project_terms(
        gathered, viewers, tile_row, columns, counts[0, 0], grad_maker, image_width, image_height
    )
    values = jnp.concatenate([feature_grad, logit_grad[None]], axis=0)
    totals = jnp.zeros((channels + 1, 2 * block_rows), jnp.float32).at[:, entries].add(values)
    returned = shifted(totals[:, block_rows:], "space", -1)
    summed = lax.psum_scatter(
        totals[:, :block_rows] + returned, "cam", scatter_dimension=1, tiled=True
    )
    return (summed[:channels], summed[channels])


def solution(mesh):
    placed = (
        P(None, ("cam", "space")),
        P(None, ("cam", "space")),
        P(("cam", "space")),
        P(("cam", "space")),
        P(),
        P(),
        P("cam", "space", None, None),
        P("cam", "space", None),
        P("cam", "space", None, None, None),
    )
    return jax.shard_map(
        on_device,
        mesh=mesh,
        in_specs=placed,
        out_specs=(P(None, ("cam", "space")), P(("cam", "space"))),
        check_vma=False,
    )
```

profile of v0, /device:TPU:4, one launch (start us, length us, event | category | flops | bytes accessed | tf_op | source)
XLA Modules:
  0.0 300.1 jit_solution(15788181093214662596)
XLA Ops:
  10.8 1.9 collective-permute-start
  12.9 10.9 %collective-permute-done = f32[69,256]{0,1:T(8,128)S(1)} collective-permute-done((f32[69,256]{0,1:T(8,128)S(1)}, f32[69,256]{0,1:T(8,128)S(1)}, u32[]{:S(2)}, u32[]{:S(2)}) %collective-permute-start) | collective-permute-done | bytes 70688 | tf_op jit(solution)/shard_map/ppermute | solution.py:12
  28.9 72.8 %all-gather.2.cloned.1.call-done = f32[2,69,4096]{1,2,0:T(8,128)} async-done(((f32[2,69,256]{1,2,0:T(8,128)}), f32[2,69,4096]{1,2,0:T(8,128)}) %all-gather.2.cloned.1.call-update) | async-done | bytes 2261008 | tf_op jit(solution)/shard_map/all_gather | solution.py:148
  101.7 2.5 slice_bitcast_fusion.1
  104.2 2.2 pad_maximum_fusion
  106.4 13.0 %gather_fusion = f32[4096,69]{1,0:T(8,128)S(1)} fusion(f32[69,8192]{0,1:T(8,128)} %pad_maximum_fusion, s32[4096]{0:T(1024)S(1)} %broadcast_clamp_fusion), kind=kCustom, calls=%fused_computation | custom fusion | bytes 2277376 | tf_op jit(solution)/shard_map/jit(_take)/gather | solution.py:154
  121.0 11.3 %while.32 = (s32[]{:T(128)}, f32[16,256]{1,0:T(8,128)S(1)}, f32[16,64,256]{2,1,0:T(8,128)S(1)}, f32[2,16,256]{2,1,0:T(8,128)S(1)}, s32[]{:T(128)}, /*index=5*/f3...) while((s32[]{:T(128)}, f32[16,256]{1,0:T(8,128)S(1)}, ...), condition=%wide.region_5.6_spmd.clone, body=%wide.region_2.5_spmd.clone.sunk | while | flops 150754048 | bytes 4895069 | solution.py:85
  123.1 2.8 multiply_convert_fusion.2
  128.7 2.8 multiply_convert_fusion.2
  134.4 4.9 %fusion.43 = bf16[16,64,256]{2,1,0:T(8,128)(2,1)S(1)} fusion(f32[16,256,512]{2,1,0:T(8,128)S(1)} %fusion.44, bf16[1,1,16,256,512]{4,3,2,1,0:T(8,128)(2,1)S(1)} %copy-done.1, bf16[64,512]{1,0:T(8,128)(2,1)S(1)} %copy-done), kind=kOutput, calls=%fused_computation.78 | convolution fusion | flops 1615069184 | bytes 13172736 | tf_op jit(solution)/shard_map/tpd,cd->tcp/dot_general | solution.py:131
  139.4 25.9 %while.33 = (s32[]{:T(128)}, f32[16,256]{1,0:T(8,128)S(1)}, f32[64,16,256]{2,0,1:T(8,128)S(1)}, f32[16,256]{1,0:T(8,128)S(1)}, s32[]{:T(128)}, /*index=5*/s32[]{...) while((s32[]{:T(128)}, f32[16,256]{1,0:T(8,128)S(1)}, ...), condition=%wide.region_11.12_spmd.clone, body=%wide.region_6.11_spmd.clone.sunk | while | flops 295195392 | bytes 27490700 | solution.py:121
  142.3 2.2 fusion.93
  144.5 2.5 fusion.92
  148.2 4.2 %fusion.95 = f32[16,128]{1,0:T(8,128)S(1)} fusion(f32[16,128,256]{2,1,0:T(8,128)S(1)} %get-tuple-element.746, f32[16,256,128]{1,0,2:T(8,128)S(1)} %fusion.94, f32[16,256]{1,0:T(8,128)S(1)} %add.491, f32[16,128]{1,0:T(8,128)S(1)} %get-tuple-element.741, f32[16,128]{1,0:T(8,128)S(1)} %get-tuple-element.742, f32[256]{0:T(256)S(1)} %fusion.90, ...), kind=kLoop, calls=%fused_computation.35.clone.1 | loop fusion | flops 8910848 | bytes 6382592 | tf_op jit(solution)/shard_map/while/body/reduce_sum | solution.py:106
  155.1 2.2 fusion.93
  157.3 2.5 fusion.92
  161.1 4.2 %fusion.95 = f32[16,128]{1,0:T(8,128)S(1)} fusion(f32[16,128,256]{2,1,0:T(8,128)S(1)} %get-tuple-element.746, f32[16,256,128]{1,0,2:T(8,128)S(1)} %fusion.94, f32[16,256]{1,0:T(8,128)S(1)} %add.491, f32[16,128]{1,0:T(8,128)S(1)} %get-tuple-element.741, f32[16,128]{1,0:T(8,128)S(1)} %get-tuple-element.742, f32[256]{0:T(256)S(1)} %fusion.90, ...), kind=kLoop, calls=%fused_computation.35.clone.1 | loop fusion | flops 8910848 | bytes 6382592 | tf_op jit(solution)/shard_map/while/body/reduce_sum | solution.py:106
  166.3 24.5 %scatter_custom_fusion = f32[65,8192]{0,1:T(8,128)} fusion(s32[4096]{0:T(1024)S(1)} %bitcast.99, f32[4096,65]{1,0:T(8,128)S(1)} %bitcast.95, f32[]{:T(128)} %constant.142.clone.1), kind=kCustom, calls=%fused_computation.75 | custom fusion | flops 266240 | bytes 2129924 | tf_op jit(solution)/shard_map/scatter-add | solution.py:160
  193.3 1.9 collective-permute-start.1
  195.2 13.7 %collective-permute-done.1 = f32[65,4096]{1,0:T(8,128)} collective-permute-done((f32[65,4096]{1,0:T(8,128)S(1)}, f32[65,4096]{1,0:T(8,128)}, u32[]{:S(2)}, u32[]{:S(2)}) %collective-permute-start.1) | collective-permute-done | bytes 1064992 | tf_op jit(solution)/shard_map/ppermute | solution.py:12
  208.9 1.8 copy.73
  210.7 3.1 %slice_add_fusion = f32[65,4096]{0,1:T(8,128)} fusion(f32[65,4096]{0,1:T(8,128)S(1)} %copy.73, f32[65,8192]{0,1:T(8,128)} %scatter_custom_fusion), kind=kLoop, calls=%fused_computation.72 | loop fusion | flops 266240 | bytes 3194880 | tf_op jit(solution)/shard_map/add | solution.py:163
  213.9 76.1 %reduce-scatter.2.cloned.1.call-done = f32[65,256]{0,1:T(8,128)} async-done(((f32[65,4096]{0,1:T(8,128)}), f32[65,256]{0,1:T(8,128)}) %reduce-scatter.2.cloned.1.call-update) | async-done | bytes 66576 | tf_op jit(solution)/shard_map/reduce_scatter | solution.py:162
  291.6 1.7 slice_reduce_fusion
  (104 shorter events, 27.9 us)
Async XLA Ops:
  7.2 125.1 %copy-start = (bf16[64,512]{1,0:T(8,128)(2,1)S(1)}, bf16[64,512]{1,0:T(8,128)(2,1)}, u32[]{:S(2)}) copy-start(bf16[64,512]{1,0:T(8,128)(2,1)} %param.18) | copy-start | bytes 196612
  7.2 17.4 %copy-start.3 = (s32[1,1,16]{2,1,0:T(1,128)S(1)}, s32[1,1,16]{2,1,0:T(1,128)}, u32[]{:S(2)}) copy-start(s32[1,1,16]{2,1,0:T(1,128)} %param.20) | copy-start | bytes 196
  7.2 18.7 %copy-start.4 = (f32[16,3]{0,1:T(4,128)S(1)}, f32[16,3]{0,1:T(4,128)}, u32[]{:S(2)}) copy-start(f32[16,3]{0,1:T(4,128)} %param.17) | copy-start | bytes 580
  7.2 20.9 %copy-start.2 = (s32[1,1,16,256]{3,2,1,0:T(8,128)S(1)}, s32[1,1,16,256]{3,2,1,0:T(8,128)}, u32[]{:S(2)}) copy-start(s32[1,1,16,256]{3,2,1,0:T(8,128)} %param.19) | copy-start | bytes 49156
  7.2 94.5 %all-gather.2.cloned.1.call-start = ((), (), s32[]{:S(2)}) async-start(), calls=%async_computation.1 | async-start | bytes 4456448 | tf_op jit(solution)/shard_map/all_gather | solution.py:148
  10.8 13.0 %collective-permute-start = (f32[69,256]{0,1:T(8,128)S(1)}, f32[69,256]{0,1:T(8,128)S(1)}, u32[]{:S(2)}, u32[]{:S(2)}) collective-permute-start(f32[69,256]{0,1:T(8,128)S(1)} %pad_maximum_fusion.2), channel_id=1, source_target_pairs={{0,1},{1,2},{2,3},{3,4},{4,5},{5,6},{6,7},{7,8},{8,9},{9,10},{10,1... | collective-permute-start | bytes 211976 | tf_op jit(solution)/shard_map/ppermute | solution.py:12
  24.5 265.5 %reduce-scatter.2.cloned.1.call-start = ((), (), s32[]{:S(2)}) async-start(), calls=%async_computation.2 | async-start | bytes 2228224 | tf_op jit(solution)/shard_map/reduce_scatter | solution.py:162
  132.2 2.2 copy-start.1
  190.8 1.6 slice-start
  193.3 15.6 %collective-permute-start.1 = (f32[65,4096]{1,0:T(8,128)S(1)}, f32[65,4096]{1,0:T(8,128)}, u32[]{:S(2)}, u32[]{:S(2)}) collective-permute-start(f32[65,4096]{1,0:T(8,128)S(1)} %copy.72), channel_id=1, source_target_pairs={{1,0},{2,1},{3,2},{4,3},{5,4},{6,5},{7,6},{8,7},{9,8},{10,9},{11,1... | collective-permute-start | bytes 3194888 | tf_op jit(solution)/shard_map/ppermute | solution.py:12
Sparse Core Ops, SparseCore 0:
  24.7 76.9 all-gather.1
  214.0 75.9 reduce-scatter.1
where the time goes:
time: 301 us; the launch traced here: 300 us
  waiting for transfers between devices  174 us (58%)
  other arithmetic  56.9 us (19%)
  local copies, waits for them, and re-layouts  31.3 us (10%)
  between operations  17.1 us (6%)
  matrix products  16.6 us (6%)
  starting transfers between devices  3.92 us (1%)
    reduce_scatter x1, waiting for transfers between devices, on_device(): lax.psum_scatter(totals[:, :block_rows] + returned, 'cam', scatter_dimens...  76.1 us
    all_gather x1, waiting for transfers between devices, on_device(): lax.all_gather(jnp.stack([own_slab, upper_slab]), 'cam', axis=2, tiled=True)  72.8 us
    ppermute x2, waiting for transfers between devices, shifted(): return lax.ppermute(shard, axis, pairs)  24.6 us
    scatter-add x1, other arithmetic, on_device(): jnp.zeros((channels + 1, 2 * block_rows), jnp.float32).at[:, entries]  24.5 us
    gather x2, local copies, waits for them, and re-layouts, on_device(): gathered = jnp.take(gauss_table, entries, axis=1)  14 us
    reduce_sum x2, other arithmetic, backward(): logit_part = logit_gate * jnp.sum(dopaque * falloff, axis=1)  8.48 us
    another operation x4, other arithmetic, block_terms(): inner_log = jnp.cumsum(log_keep, axis=2) - log_keep  8.17 us
  transfers between devices with their start and end apart: 4, of which 4 were waited for; matrix products, arithmetic and copies ran while one was open for 1% of the time, Pallas kernels for 0%

commit v1 on v0

--- a/solution.py
+++ b/solution.py
@@ -145,7 +145,12 @@
     block_rows = camera_count * length
     own_slab = jnp.concatenate([features, positions, spreads[None], logits[None]], axis=0)
     upper_slab = shifted(own_slab, "space", 1)
-    both_slabs = lax.all_gather(jnp.stack([own_slab, upper_slab]), "cam", axis=2, tiled=True)
+    both_slabs = jnp.concatenate(
+        lax.all_to_all(
+            jnp.stack([jnp.stack([own_slab, upper_slab])] * lax.axis_size("cam")), "cam", 0, 0
+        ),
+        axis=2,
+    )
     gauss_table = jnp.concatenate([both_slabs[0], both_slabs[1]], axis=1)
     entries = tile_lists[0, 0]
     picker = (jnp.arange(camera_count, dtype=jnp.int32) == camera_id).astype(jnp.float32)

time: 301 us -> 289 us (0.960)
  waiting for transfers between devices: 174 us -> 145 us
  starting transfers between devices: 3.92 us -> 16 us
  local copies, waits for them, and re-layouts: 31.3 us -> 35.2 us
    all_gather x1 -> x0, waiting for transfers between devices: 72.8 us -> none  [on_device(): lax.all_gather(jnp.stack([own_slab, upper_slab]), 'cam', axis=2, tiled=True)]
    all_to_all x0 -> x1, waiting for transfers between devices: none -> 41.9 us  [on_device(): lax.all_to_all(jnp.stack([jnp.stack([own_slab, upper_slab])] * lax.axis_s...]
    all_to_all x0 -> x1, starting transfers between devices: none -> 8.87 us  [on_device(): lax.all_to_all(jnp.stack([jnp.stack([own_slab, upper_slab])] * lax.axis_s...]
    slice x0 -> x3, local copies, waits for them, and re-layouts: none -> 7.67 us  [on_device(): gauss_table = jnp.concatenate([both_slabs[0], both_slabs[1]], axis=1)]
    ppermute x2, starting transfers between devices: 3.84 us -> 7.11 us  [shifted(): return lax.ppermute(shard, axis, pairs)]
where the time goes in v1:
time: 289 us
  waiting for transfers between devices  145 us (50%)
  other arithmetic  58.4 us (20%)
  local copies, waits for them, and re-layouts  35.2 us (12%)
  between operations  16.9 us (6%)
  matrix products  16.6 us (6%)
  starting transfers between devices  16 us (6%)
    reduce_scatter x1, waiting for transfers between devices, on_device(): lax.psum_scatter(totals[:, :block_rows] + returned, 'cam', scatter_dimens...  78.8 us
    all_to_all x1, waiting for transfers between devices, on_device(): lax.all_to_all(jnp.stack([jnp.stack([own_slab, upper_slab])] * lax.axis_s...  41.9 us
    scatter-add x1, other arithmetic, on_device(): jnp.zeros((channels + 1, 2 * block_rows), jnp.float32).at[:, entries]  24.5 us
    ppermute x2, waiting for transfers between devices, shifted(): return lax.ppermute(shard, axis, pairs)  24.1 us
    gather x2, local copies, waits for them, and re-layouts, on_device(): gathered = jnp.take(gauss_table, entries, axis=1)  14 us
    all_to_all x1, starting transfers between devices, on_device(): lax.all_to_all(jnp.stack([jnp.stack([own_slab, upper_slab])] * lax.axis_s...  8.87 us
    reduce_sum x2, other arithmetic, backward(): logit_part = logit_gate * jnp.sum(dopaque * falloff, axis=1)  8.48 us
    another operation x4, other arithmetic, block_terms(): inner_log = jnp.cumsum(log_keep, axis=2) - log_keep  8.17 us
  transfers between devices with their start and end apart: 4, of which 4 were waited for; matrix products, arithmetic and copies ran while one was open for 1% of the time, Pallas kernels for 0%

profile of v1, /device:TPU:4, one launch (start us, length us, event | category | flops | bytes accessed | tf_op | source)
XLA Modules:
  0.0 288.5 jit_solution(18108499151227215452)
XLA Ops:
  10.0 10.4 %collective-permute-done = f32[69,256]{1,0:T(8,128)S(1)} collective-permute-done((f32[69,256]{1,0:T(8,128)S(1)}, f32[69,256]{1,0:T(8,128)S(1)}, u32[]{:S(2)}, u32[]{:S(2)}) %collective-permute-start) | collective-permute-done | bytes 70688 | tf_op jit(solution)/shard_map/ppermute | solution.py:12
  22.6 8.9 %all-to-all-start = ((f32[16,2,69,256]{3,1,2,0:T(2,128)}), f32[16,2,69,256]{3,1,2,0:T(2,128)S(1)}, u32[]{:S(2)}, u32[]{:S(2)}) async-start(f32[16,2,69,256]{3,1,2,0:T(2,128)} %stack.11), calls=%async_computation | async-start | bytes 4521984 | tf_op jit(solution)/shard_map/all_to_all | solution.py:149
  35.7 41.9 %all-to-all-done = f32[16,2,69,256]{3,1,2,0:T(2,128)S(1)} async-done(((f32[16,2,69,256]{3,1,2,0:T(2,128)}), f32[16,2,69,256]{3,1,2,0:T(2,128)S(1)}, u32[]{:S(2)}, u32[]{:S(2)}) %all-to-all-start) | async-done | bytes 2261024 | tf_op jit(solution)/shard_map/all_to_all | solution.py:149
  77.6 2.7 fusion.63
  80.3 2.6 copy.54
  82.9 2.4 copy.55
  85.2 3.8 %pad_maximum_fusion = f32[69,8192]{0,1:T(8,128)} fusion(f32[69,4096]{0,1:T(8,128)} %bitcast.95, f32[69,4096]{0,1:T(8,128)S(1)} %bitcast.94), kind=kLoop, calls=%fused_computation.70 | loop fusion | flops 565248 | bytes 4521984 | tf_op jit(solution)/shard_map/concatenate | solution.py:154
  89.0 13.0 %gather_fusion = f32[4096,69]{1,0:T(8,128)S(1)} fusion(f32[69,8192]{0,1:T(8,128)} %pad_maximum_fusion, s32[4096]{0:T(1024)S(1)} %broadcast_clamp_fusion), kind=kCustom, calls=%fused_computation | custom fusion | bytes 2277376 | tf_op jit(solution)/shard_map/jit(_take)/gather | solution.py:159
  103.6 11.3 %while.32 = (s32[]{:T(128)}, f32[16,256]{1,0:T(8,128)S(1)}, f32[16,64,256]{2,1,0:T(8,128)S(1)}, f32[2,16,256]{2,1,0:T(8,128)S(1)}, s32[]{:T(128)}, /*index=5*/f3...) while((s32[]{:T(128)}, f32[16,256]{1,0:T(8,128)S(1)}, ...), condition=%wide.region_5.6_spmd.clone, body=%wide.region_2.5_spmd.clone.sunk | while | flops 150754048 | bytes 4895069 | solution.py:85
  105.8 2.8 multiply_convert_fusion.2
  111.3 2.8 multiply_convert_fusion.2
  117.1 4.9 %fusion.43 = bf16[16,64,256]{2,1,0:T(8,128)(2,1)S(1)} fusion(f32[16,256,512]{2,1,0:T(8,128)S(1)} %fusion.44, bf16[1,1,16,256,512]{4,3,2,1,0:T(8,128)(2,1)S(1)} %copy-done.1, bf16[64,512]{1,0:T(8,128)(2,1)S(1)} %copy-done), kind=kOutput, calls=%fused_computation.76 | convolution fusion | flops 1615069184 | bytes 13172736 | tf_op jit(solution)/shard_map/tpd,cd->tcp/dot_general | solution.py:131
  122.1 25.7 %while.33 = (s32[]{:T(128)}, f32[16,256]{1,0:T(8,128)S(1)}, f32[64,16,256]{2,0,1:T(8,128)S(1)}, f32[16,256]{1,0:T(8,128)S(1)}, s32[]{:T(128)}, /*index=5*/s32[]{...) while((s32[]{:T(128)}, f32[16,256]{1,0:T(8,128)S(1)}, ...), condition=%wide.region_11.12_spmd.clone, body=%wide.region_6.11_spmd.clone.sunk | while | flops 295195392 | bytes 27490700 | solution.py:121
  124.7 2.2 fusion.94
  126.9 2.5 fusion.93
  130.7 4.2 %fusion.96 = f32[16,128]{1,0:T(8,128)S(1)} fusion(f32[16,128,256]{2,1,0:T(8,128)S(1)} %get-tuple-element.748, f32[16,256,128]{1,0,2:T(8,128)S(1)} %fusion.95, f32[16,256]{1,0:T(8,128)S(1)} %add.491, f32[16,128]{1,0:T(8,128)S(1)} %get-tuple-element.743, f32[16,128]{1,0:T(8,128)S(1)} %get-tuple-element.744, f32[256]{0:T(256)S(1)} %fusion.91, ...), kind=kLoop, calls=%fused_computation.35.clone.1 | loop fusion | flops 8910848 | bytes 6382592 | tf_op jit(solution)/shard_map/while/body/reduce_sum | solution.py:106
  137.5 2.2 fusion.94
  139.7 2.5 fusion.93
  143.5 4.2 %fusion.96 = f32[16,128]{1,0:T(8,128)S(1)} fusion(f32[16,128,256]{2,1,0:T(8,128)S(1)} %get-tuple-element.748, f32[16,256,128]{1,0,2:T(8,128)S(1)} %fusion.95, f32[16,256]{1,0:T(8,128)S(1)} %add.491, f32[16,128]{1,0:T(8,128)S(1)} %get-tuple-element.743, f32[16,128]{1,0:T(8,128)S(1)} %get-tuple-element.744, f32[256]{0:T(256)S(1)} %fusion.91, ...), kind=kLoop, calls=%fused_computation.35.clone.1 | loop fusion | flops 8910848 | bytes 6382592 | tf_op jit(solution)/shard_map/while/body/reduce_sum | solution.py:106
  148.8 24.5 %scatter_custom_fusion = f32[65,8192]{0,1:T(8,128)} fusion(s32[4096]{0:T(1024)S(1)} %bitcast.101, f32[4096,65]{1,0:T(8,128)S(1)} %bitcast.97, f32[]{:T(128)} %constant.142.clone.1), kind=kCustom, calls=%fused_computation.73 | custom fusion | flops 266240 | bytes 2129924 | tf_op jit(solution)/shard_map/scatter-add | solution.py:165
  175.7 5.2 %collective-permute-start.1 = (f32[65,4096]{1,0:T(8,128)S(1)}, f32[65,4096]{1,0:T(8,128)}, u32[]{:S(2)}, u32[]{:S(2)}) collective-permute-start(f32[65,4096]{1,0:T(8,128)S(1)} %copy.67), channel_id=1, source_target_pairs={{1,0},{2,1},{3,2},{4,3},{5,4},{6,5},{7,6},{8,7},{9,8},{10,9},{11,1... | collective-permute-start | bytes 3194888 | tf_op jit(solution)/shard_map/ppermute | solution.py:12
  180.9 13.7 %collective-permute-done.1 = f32[65,4096]{1,0:T(8,128)} collective-permute-done((f32[65,4096]{1,0:T(8,128)S(1)}, f32[65,4096]{1,0:T(8,128)}, u32[]{:S(2)}, u32[]{:S(2)}) %collective-permute-start.1) | collective-permute-done | bytes 1064992 | tf_op jit(solution)/shard_map/ppermute | solution.py:12
  196.4 3.1 %slice_add_fusion = f32[65,4096]{0,1:T(8,128)} fusion(f32[65,4096]{0,1:T(8,128)S(1)} %copy.68, f32[65,8192]{0,1:T(8,128)} %scatter_custom_fusion), kind=kLoop, calls=%fused_computation.72 | loop fusion | flops 266240 | bytes 3194880 | tf_op jit(solution)/shard_map/add | solution.py:168
  199.6 78.8 %reduce-scatter.2.cloned.1.call-done = f32[65,256]{0,1:T(8,128)} async-done(((f32[65,4096]{0,1:T(8,128)}), f32[65,256]{0,1:T(8,128)}) %reduce-scatter.2.cloned.1.call-update) | async-done | bytes 66576 | tf_op jit(solution)/shard_map/reduce_scatter | solution.py:167
  (102 shorter events, 31.8 us)
Async XLA Ops:
  7.2 107.7 %copy-start = (bf16[64,512]{1,0:T(8,128)(2,1)S(1)}, bf16[64,512]{1,0:T(8,128)(2,1)}, u32[]{:S(2)}) copy-start(bf16[64,512]{1,0:T(8,128)(2,1)} %param.18) | copy-start | bytes 196612
  8.1 12.4 %collective-permute-start = (f32[69,256]{1,0:T(8,128)S(1)}, f32[69,256]{1,0:T(8,128)S(1)}, u32[]{:S(2)}, u32[]{:S(2)}) collective-permute-start(f32[69,256]{1,0:T(8,128)S(1)} %get-tuple-element.528), channel_id=1, source_target_pairs={{0,1},{1,2},{2,3},{3,4},{4,5},{5,6},{6,7},{7,8},{8,9},{9,10},{10,1... | collective-permute-start | bytes 211976 | tf_op jit(solution)/shard_map/ppermute | solution.py:12
  22.5 8.9 %copy-start.3 = (s32[1,1,16]{2,1,0:T(1,128)S(1)}, s32[1,1,16]{2,1,0:T(1,128)}, u32[]{:S(2)}) copy-start(s32[1,1,16]{2,1,0:T(1,128)} %param.20) | copy-start | bytes 196
  22.5 10.3 %copy-start.4 = (f32[16,3]{0,1:T(4,128)S(1)}, f32[16,3]{0,1:T(4,128)}, u32[]{:S(2)}) copy-start(f32[16,3]{0,1:T(4,128)} %param.17) | copy-start | bytes 580
  22.6 12.4 %copy-start.2 = (s32[1,1,16,256]{3,2,1,0:T(8,128)S(1)}, s32[1,1,16,256]{3,2,1,0:T(8,128)}, u32[]{:S(2)}) copy-start(s32[1,1,16,256]{3,2,1,0:T(8,128)} %param.19) | copy-start | bytes 49156
  22.6 55.0 %all-to-all-start = ((f32[16,2,69,256]{3,1,2,0:T(2,128)}), f32[16,2,69,256]{3,1,2,0:T(2,128)S(1)}, u32[]{:S(2)}, u32[]{:S(2)}) async-start(f32[16,2,69,256]{3,1,2,0:T(2,128)} %stack.11), calls=%async_computation | async-start | bytes 4521984 | tf_op jit(solution)/shard_map/all_to_all | solution.py:149
  31.4 247.0 %reduce-scatter.2.cloned.1.call-start = ((), (), s32[]{:S(2)}) async-start(), calls=%async_computation.2 | async-start | bytes 2228224 | tf_op jit(solution)/shard_map/reduce_scatter | solution.py:167
  114.9 2.2 copy-start.1
  173.2 1.6 slice-start
  175.7 18.9 %collective-permute-start.1 = (f32[65,4096]{1,0:T(8,128)S(1)}, f32[65,4096]{1,0:T(8,128)}, u32[]{:S(2)}, u32[]{:S(2)}) collective-permute-start(f32[65,4096]{1,0:T(8,128)S(1)} %copy.67), channel_id=1, source_target_pairs={{1,0},{2,1},{3,2},{4,3},{5,4},{6,5},{7,6},{8,7},{9,8},{10,9},{11,1... | collective-permute-start | bytes 3194888 | tf_op jit(solution)/shard_map/ppermute | solution.py:12
Sparse Core Ops, SparseCore 0:
  199.7 78.6 reduce-scatter.1
